TPU v7x, 32 devices: a whole 2x2x4 slice. The times are simulated.
32 devices in a mesh: leaf: 2 (over x), rows: 16 (over z, y, core).
Axes of the slice: x: 2, y: 2, z: 4, core: 2. Of those that a mesh axis runs over, the one named last changes fastest.
Arguments:
- features: bfloat16 [262144, 256], P(('leaf', 'rows')), parts along dimension 0, may hold values from -80 to 80
- node_ids: int32 [262144], P(('leaf', 'rows')), parts along dimension 0, may hold values from -1 to 15, as said below
- labels: int32 [262144], P(('leaf', 'rows')), parts along dimension 0, may hold values from 0 to 15
- owners: int32 [32], P('leaf'), parts along dimension 0, may hold values from 0 to 15, each once
Outputs:
- hyperplanes: float32 [32, 16, 256], P(('leaf', 'rows')), parts along dimension 0
- scores: float32 [16, 262144], P(None, ('leaf', 'rows')), parts along dimension 1
There are 2 independent parts, one for each index of `leaf`. A program takes and returns all parts, laid end to end along the dimension named above; each array names one. Nothing has to cross between parts.
Inputs may be any that keep to these rules, and one draw needn't show every extreme that they name: `node_ids`: on rows device d, row p of node n's segment (local row n * 512 + p) holds n or -1; the live rows of a segment come first and there is at least one; some segment of every device is full. Each node number appears once in owners; node n is owned by the device of rows with index owners[n].
All inputs are finite; a program needn't handle non-finite values.
Results may differ from a plain program's by a relative error of at most 0.0035.
Values may be sent and summed in bfloat16 or wider, within the bound.
A program may use at most 128 MiB of HBM per device.

v0:
```python
import jax
import jax.numpy as jnp
from jax import lax
from jax.sharding import PartitionSpec as P

CLASSES = 16
ridge_term = 0.1


def solve_nodes(scatter, sums, counts):
    totals = jnp.sum(counts, axis=1)
    centers = jnp.sum(sums, axis=1) / totals[:, None]
    scaled = sums / jnp.maximum(counts, 1.0)[:, :, None]
    within = scatter - jnp.einsum("ncf,ncg->nfg", scaled, sums, precision=lax.Precision.HIGHEST)
    identity = jnp.eye(scatter.shape[-1], dtype=jnp.float32)
    system = within / totals[:, None, None] + ridge_term * identity
    shifts = (sums - counts[:, :, None] * centers[:, None, :]) / totals[:, None, None]
    factor = jnp.linalg.cholesky(system)
    planes = jax.vmap(lambda lower, right: jax.scipy.linalg.cho_solve((lower, True), right.T).T)(
        factor, shifts
    )
    offsets = -jnp.einsum("ncf,nf->nc", planes, centers, precision=lax.Precision.HIGHEST)
    return (planes, offsets)


def on_device(features, node_ids, labels, owners):
    row_count, feature_count = features.shape
    node_count = owners.shape[0]
    segment = row_count // node_count
    inverse = (
        jnp.zeros((node_count,), jnp.int32).at[owners].set(jnp.arange(node_count, dtype=jnp.int32))
    )
    blocks = jnp.take(features.reshape(node_count, segment, feature_count), inverse, axis=0)
    slot_ids = jnp.take(node_ids.reshape(node_count, segment), inverse, axis=0)
    marks = jnp.take(labels.reshape(node_count, segment), inverse, axis=0)
    live_rows = slot_ids == inverse[:, None]
    masked = jnp.where(live_rows[:, :, None], blocks, jnp.zeros((), jnp.bfloat16))
    classes = jnp.arange(CLASSES, dtype=jnp.int32)
    tagged = jnp.where(live_rows, marks, -1).astype(jnp.bfloat16)
    arrived, arrived_tags = (
        lax.all_to_all(masked, "rows", split_axis=0, concat_axis=1, tiled=True),
        lax.all_to_all(tagged, "rows", split_axis=0, concat_axis=1, tiled=True),
    )
    owner_tags = arrived_tags.astype(jnp.int32)
    owner_hot = (owner_tags[:, None, :] == classes[None, :, None]).astype(jnp.bfloat16)
    mine_sums = jnp.einsum("ncs,nsf->ncf", owner_hot, arrived, preferred_element_type=jnp.float32)
    mine_counts = jnp.sum(owner_hot.astype(jnp.float32), axis=2)
    scatter = jnp.einsum("nsf,nsg->nfg", arrived, arrived, preferred_element_type=jnp.float32)
    planes, offsets = solve_nodes(scatter, mine_sums, mine_counts)
    every_planes, every_offsets = (
        lax.all_gather(planes, "rows", axis=0, tiled=True),
        lax.all_gather(offsets, "rows", axis=0, tiled=True),
    )
    rounded = every_planes.astype(jnp.bfloat16)
    result = jnp.einsum("ncf,nsf->cns", rounded, blocks, preferred_element_type=jnp.float32)
    result = result + every_offsets.T[:, :, None]
    result = jnp.where(live_rows[None], result, 0.0)
    result = jnp.take(result, owners, axis=1).reshape(CLASSES, row_count)
    return (planes, result)


def solution(mesh):
    in_specs = (P(("leaf", "rows"), None), P(("leaf", "rows")), P(("leaf", "rows")), P("leaf"))
    out_specs = (P(("leaf", "rows"), None, None), P(None, ("leaf", "rows")))
    return jax.shard_map(
        on_device, mesh=mesh, in_specs=in_specs, out_specs=out_specs, check_vma=False
    )
```

profile of v0, /device:TPU:0, one launch (start us, length us, event | category | flops | bytes accessed | tf_op | source)
XLA Modules:
  0.0 252.2 jit_solution(4196847479306877663)
XLA Ops:
  0.6 0.7 compare_select_fusion.1
  1.3 0.6 scatter_custom_fusion
  1.9 0.7 compare_and_fusion
  2.6 0.8 reshape.307
  3.4 0.8 reshape.309
  5.9 0.7 reduce.23
  6.6 0.6 reshape.402
  7.2 7.4 %all-to-all-start.1 = ((bf16[16,2,256]{2,1,0:T(2,128)(2,1)}), bf16[16,2,256]{2,1,0:T(2,128)(2,1)S(1)}, u32[]{:S(2)}, u32[]{:S(2)}) async-start(bf16[16,2,256]{2,1,0:T(2,128)(2,1)} %reshape.402), calls=%async_computation.1 | async-start | bytes 32768 | tf_op jit(solution)/shard_map/all_to_all | solution.py:42
  14.6 4.9 %gather_fusion = bf16[16,512,256]{2,1,0:T(8,128)(2,1)} fusion(bf16[16,512,256]{2,1,0:T(8,128)(2,1)} %bitcast.110, s32[1024]{0:T(1024)S(1)} %pad_clamp_fusion.1), kind=kCustom, calls=%fused_computation.2 | custom fusion | bytes 8388672 | tf_op jit(solution)/shard_map/jit(_take)/gather | solution.py:33
  19.5 5.3 %broadcast_select_fusion.1 = bf16[16,512,256]{2,1,0:T(8,128)(2,1)} fusion(pred[16,512]{1,0:T(8,128)(4,1)S(1)} %get-tuple-element.24, bf16[16,512,256]{2,1,0:T(8,128)(2,1)} %gather_fusion, pred[16]{0:T(512)(128)(4,1)S(1)} %get-tuple-element.35), kind=kLoop, calls=%fused_computation.8 | loop fusion | flops 4194304 | bytes 8396816 | tf_op jit(solution)/shard_map/jit(_where)/select_n | solution.py:37
  24.8 6.2 %all-to-all-start = ((bf16[16,512,256]{2,1,0:T(8,128)(2,1)}), bf16[16,512,256]{2,1,0:T(8,128)(2,1)}, u32[]{:S(2)}, u32[]{:S(2)}) async-start(bf16[16,512,256]{2,1,0:T(8,128)(2,1)} %broadcast_select_fusion.1), calls=%async_computation | async-start | bytes 8388608 | tf_op jit(solution)/shard_map/all_to_all | solution.py:41
  32.5 0.8 convert_reduce_fusion.1
  33.2 75.3 %all-to-all-done = bf16[16,512,256]{2,1,0:T(8,128)(2,1)} async-done(((bf16[16,512,256]{2,1,0:T(8,128)(2,1)}), bf16[16,512,256]{2,1,0:T(8,128)(2,1)}, u32[]{:S(2)}, u32[]{:S(2)}) %all-to-all-start) | async-done | bytes 4194336 | tf_op jit(solution)/shard_map/all_to_all | solution.py:41
  108.5 2.9 %fusion.33 = (f32[256]{0:T(256)S(1)}, f32[16,256]{1,0:T(8,128)S(1)}) fusion(bf16[8192,256]{1,0:T(8,128)(2,1)} %bitcast.4, s32[8192]{0:T(1024)S(1)} %bitcast.115), kind=kOutput, calls=%fused_computation.85 | convolution fusion | flops 67243776 | bytes 4244480 | tf_op jit(solution)/shard_map/ncs,nsf->ncf/dot_general | solution.py:46
  111.4 0.7 broadcast_divide_fusion
  112.1 0.7 divide_bitcast_fusion
  112.8 5.2 %convolution_bitcast_fusion = f32[256,256]{0,1:T(8,128)S(1)} fusion(bf16[16,512,256]{2,1,0:T(8,128)(2,1)} %all-to-all-done), kind=kOutput, calls=%fused_computation.16 | convolution fusion | flops 1073741824 | bytes 4456448 | tf_op jit(solution)/shard_map/nsf,nsg->nfg/dot_general | solution.py:48
  118.0 1.1 fusion.5
  119.3 11.7 %custom-call.20 = f32[1,128,128]{2,1,0:T(8,128)S(1)} custom-call(f32[1,128,128]{2,1,0:T(8,128)S(1)} %cholesky.117), custom_call_target="Cholesky" | custom-call | tf_op jit(solution)/shard_map/jit(cholesky)/cholesky | solution.py:18
  131.0 9.8 %custom-call.21 = f32[1,1,128,128]{2,3,1,0:T(8,128)S(1)} custom-call(f32[1,1,128,128]{3,2,1,0:T(8,128)S(1)} %get-tuple-element.30), custom_call_target="InvertDiagBlocksLowerTriangular" | custom-call | tf_op jit(solution)/shard_map/jit(cholesky)/cholesky | solution.py:18
  141.3 11.9 %custom-call.22 = f32[1,128,128]{2,1,0:T(8,128)S(1)} custom-call(f32[1,128,128]{2,1,0:T(8,128)S(1)} %fusion.6), custom_call_target="Cholesky" | custom-call | tf_op jit(solution)/shard_map/jit(cholesky)/cholesky | solution.py:18
  153.3 0.6 compare_reduce_fusion
  153.9 0.6 compare_reduce_fusion.1
  155.9 3.9 %while.1 = (s32[]{:T(128)}, f32[1,256,256]{2,1,0:T(8,128)S(1)}, s32[2,2]{1,0:T(2,128)S(1)}, f32[2,1,128,128]{3,2,1,0:T(8,128)S(1)}, s32[]{:T(128)}) while((s32[]{:T(128)}, f32[1,256,256]{2,1,0:T(8,128)S(1)}, s32[2,2]{1,0:T(2,128)S(1)}, f32[2,1,128,128]{3,2,1,0:T(8,128)S(1)}, s32[]{:T(128)}) %tuple.32), condition=%wide.while_cond, body=%wide.while_body.sunk | while | flops 2 | bytes 131181 | solution.py:19
  156.5 1.4 bitcast_dynamic-update-slice_fusion.3
  158.5 1.4 bitcast_dynamic-update-slice_fusion.3
  159.9 19.7 %custom-call.23 = f32[1,2,128,128]{2,3,1,0:T(8,128)S(1)} custom-call(f32[1,2,128,128]{3,2,1,0:T(8,128)S(1)} %bitcast.121), custom_call_target="InvertDiagBlocksLowerTriangular" | custom-call | tf_op jit(solution)/shard_map/vmap(jit(_cho_solve))/triangular_solve | solution.py:19
  180.7 0.7 fusion.30
  181.3 35.7 %all_gather.6 = bf16[16,16,256]{2,1,0:T(8,128)(2,1)S(1)} all-gather(bf16[1,16,256]{2,1,0:T(8,128)(2,1)S(1)} %get-tuple-element.21), channel_id=1, replica_groups=mesh['leaf'=2,'rows'=16] {'rows'}, dimensions={0}, use_global_device_ids=true | all-gather | bytes 139264 | tf_op jit(solution)/shard_map/all_gather | solution.py:51
  217.4 29.8 %all-reduce.1 = f32[256]{0:T(256)S(1)} all-reduce(f32[256]{0:T(256)S(1)} %dynamic-update-slice.11), channel_id=2, replica_groups=mesh['leaf'=2,'rows'=16] {'rows'}, use_global_device_ids=true, to_apply=%add.1 | all-reduce | flops 256 | bytes 2048
  247.2 3.4 %fusion.3 = f32[16,16,512]{2,0,1:T(8,128)S(1)} fusion(bf16[16,512,256]{2,1,0:T(8,128)(2,1)} %gather_fusion, pred[16]{0:T(512)(128)(4,1)S(1)} %get-tuple-element.35, f32[16,16]{0,1:T(8,128)S(1)} %bitcast.120, pred[16,512]{1,0:T(8,128)(4,1)S(1)} %get-tuple-element.24, bf16[16,16,256]{2,1,0:T(8,128)(2,1)S(1)} %all_gather.6), kind=kOutput, calls=%fused_computation.12 | convolution fusion | flops 69468160 | bytes 4858896 | tf_op jit(solution)/shard_map/ncf,nsf->cns/dot_general | solution.py:55
  251.4 0.8 broadcast_select_fusion.9
  (45 shorter events, 6.7 us)
Async XLA Ops:
  7.2 17.6 %all-to-all-start.1 = ((bf16[16,2,256]{2,1,0:T(2,128)(2,1)}), bf16[16,2,256]{2,1,0:T(2,128)(2,1)S(1)}, u32[]{:S(2)}, u32[]{:S(2)}) async-start(bf16[16,2,256]{2,1,0:T(2,128)(2,1)} %reshape.402), calls=%async_computation.1 | async-start | bytes 32768 | tf_op jit(solution)/shard_map/all_to_all | solution.py:42
  24.8 6.3 %copy-start = (u32[32]{0:T(128)S(1)}, u32[32]{0:T(128)}, u32[]{:S(2)}) copy-start(u32[32]{0:T(128)} %constant.166) | copy-start | bytes 388
  24.8 83.7 %all-to-all-start = ((bf16[16,512,256]{2,1,0:T(8,128)(2,1)}), bf16[16,512,256]{2,1,0:T(8,128)(2,1)}, u32[]{:S(2)}, u32[]{:S(2)}) async-start(bf16[16,512,256]{2,1,0:T(8,128)(2,1)} %broadcast_select_fusion.1), calls=%async_computation | async-start | bytes 8388608 | tf_op jit(solution)/shard_map/all_to_all | solution.py:41
where the time goes:
time: 253 us; the launch traced here: 252 us
  waiting for transfers between devices  75.3 us (30%)
  other arithmetic  65.5 us (26%)
  blocking collectives  65.5 us (26%)
  local copies, waits for them, and re-layouts  15.1 us (6%)
  matrix products  14.3 us (6%)
  starting transfers between devices  13.6 us (5%)
  between operations  2.8 us (1%)
    all_to_all x1, waiting for transfers between devices, on_device(): lax.all_to_all(masked, 'rows', split_axis=0, concat_axis=1, tiled=True)  75.3 us
    all_gather x1, blocking collectives, on_device(): lax.all_gather(planes, 'rows', axis=0, tiled=True)  35.7 us
    another operation x7, other arithmetic, solve_nodes(): factor = jnp.linalg.cholesky(system)  34.8 us
    unnamed x1, blocking collectives  29.8 us
    another operation x3, other arithmetic, solve_nodes(): jax.scipy.linalg.cho_solve((lower, True), right.T)  19.7 us
    all_to_all x1, starting transfers between devices, on_device(): lax.all_to_all(tagged, 'rows', split_axis=0, concat_axis=1, tiled=True)  7.41 us
    all_to_all x1, starting transfers between devices, on_device(): lax.all_to_all(masked, 'rows', split_axis=0, concat_axis=1, tiled=True)  6.19 us
    select_n x1, other arithmetic, on_device(): jnp.where(live_rows[:, :, None], blocks, jnp.zeros((), jnp.bfloat16))  5.27 us
  transfers between devices with their start and end apart: 2, of which 1 were waited for; matrix products, arithmetic and copies ran while one was open for 5% of the time, Pallas kernels for 0%

commit v1 on v0

--- a/solution.py
+++ b/solution.py
@@ -38,7 +38,12 @@
     classes = jnp.arange(CLASSES, dtype=jnp.int32)
     tagged = jnp.where(live_rows, marks, -1).astype(jnp.bfloat16)
     arrived, arrived_tags = (
-        lax.all_to_all(masked, "rows", split_axis=0, concat_axis=1, tiled=True),
+        jnp.concatenate(
+            lax.all_to_all(
+                jnp.stack(jnp.split(masked, lax.axis_size("rows"), axis=0)), "rows", 0, 0
+            ),
+            axis=1,
+        ),
         lax.all_to_all(tagged, "rows", split_axis=0, concat_axis=1, tiled=True),
     )
     owner_tags = arrived_tags.astype(jnp.int32)

time: 253 us -> 263 us (1.040)
  local copies, waits for them, and re-layouts: 15.1 us -> 26.7 us
    unnamed x9 -> x24, local copies, waits for them, and re-layouts: 1.53 us -> 12.4 us
  transfers between devices with their start and end apart: 2 -> 2, of which waited for: 1 -> 1; matrix products, arithmetic and copies ran while one was open for 5% -> 8% of each run, Pallas kernels for 0% -> 0%
where the time goes in v1:
time: 263 us; the launch traced here: 262 us
  waiting for transfers between devices  75.3 us (29%)
  blocking collectives  65.5 us (25%)
  other arithmetic  63.9 us (24%)
  local copies, waits for them, and re-layouts  26.7 us (10%)
  matrix products  14.3 us (5%)
  starting transfers between devices  13.6 us (5%)
  between operations  2.81 us (1%)
    all_to_all x1, waiting for transfers between devices, on_device(): lax.all_to_all(jnp.stack(jnp.split(masked, lax.axis_size('rows'), axis=0)...  75.3 us
    all_gather x1, blocking collectives, on_device(): lax.all_gather(planes, 'rows', axis=0, tiled=True)  35.7 us
    another operation x7, other arithmetic, solve_nodes(): factor = jnp.linalg.cholesky(system)  34.8 us
    unnamed x1, blocking collectives  29.8 us
    another operation x3, other arithmetic, solve_nodes(): jax.scipy.linalg.cho_solve((lower, True), right.T)  19.7 us
    unnamed x24, local copies, waits for them, and re-layouts  12.4 us
    all_to_all x1, starting transfers between devices, on_device(): lax.all_to_all(tagged, 'rows', split_axis=0, concat_axis=1, tiled=True)  7.41 us
    all_to_all x1, starting transfers between devices, on_device(): lax.all_to_all(jnp.stack(jnp.split(masked, lax.axis_size('rows'), axis=0)...  6.19 us
  transfers between devices with their start and end apart: 2, of which 1 were waited for; matrix products, arithmetic and copies ran while one was open for 8% of the time, Pallas kernels for 0%

profile of v1, /device:TPU:0, one launch (start us, length us, event | category | flops | bytes accessed | tf_op | source)
XLA Modules:
  0.0 262.2 jit_solution(5947443666818444721)
XLA Ops:
  2.6 0.8 reshape.309
  3.4 0.8 reshape.312
  7.2 7.4 %all-to-all-start.1 = ((bf16[16,2,256]{2,1,0:T(2,128)(2,1)}), bf16[16,2,256]{2,1,0:T(2,128)(2,1)S(1)}, u32[]{:S(2)}, u32[]{:S(2)}) async-start(bf16[16,2,256]{2,1,0:T(2,128)(2,1)} %reshape.405), calls=%async_computation.1 | async-start | bytes 32768 | tf_op jit(solution)/shard_map/all_to_all | solution.py:47
  14.6 4.9 %gather_fusion = bf16[16,512,256]{2,1,0:T(8,128)(2,1)} fusion(bf16[16,512,256]{2,1,0:T(8,128)(2,1)} %bitcast.177, s32[1024]{0:T(1024)S(1)} %pad_clamp_fusion.1), kind=kCustom, calls=%fused_computation.2 | custom fusion | bytes 8388672 | tf_op jit(solution)/shard_map/jit(_take)/gather | solution.py:33
  19.5 3.6 %broadcast_select_fusion.1 = bf16[16,512,256]{2,1,0:T(8,128)(2,1)S(1)} fusion(pred[16,512]{1,0:T(8,128)(4,1)S(1)} %get-tuple-element.24, bf16[16,512,256]{2,1,0:T(8,128)(2,1)} %gather_fusion, pred[16]{0:T(512)(128)(4,1)S(1)} %get-tuple-element.35), kind=kLoop, calls=%fused_computation.10 | loop fusion | flops 4194304 | bytes 8396816 | tf_op jit(solution)/shard_map/jit(_where)/select_n | solution.py:37
  23.1 0.7 fusion.32
  24.6 0.7 fusion.30
  25.3 0.7 fusion.29
  26.8 0.7 fusion.27
  27.5 0.7 fusion.26
  28.3 0.7 fusion.25
  29.0 0.7 fusion.24
  29.7 0.7 fusion.23
  30.5 0.7 fusion.22
  34.0 0.7 fusion.17
  34.8 6.2 %all-to-all-start = ((bf16[16,1,512,256]{3,2,1,0:T(8,128)(2,1)}), bf16[16,1,512,256]{3,2,1,0:T(8,128)(2,1)}, u32[]{:S(2)}, u32[]{:S(2)}) async-start(bf16[16,1,512,256]{3,2,1,0:T(8,128)(2,1)} %fusion.17), calls=%async_computation | async-start | bytes 8388608 | tf_op jit(solution)/shard_map/all_to_all | solution.py:42
  42.4 0.8 convert_reduce_fusion.1
  43.2 75.3 %all-to-all-done = bf16[16,1,512,256]{3,2,1,0:T(8,128)(2,1)} async-done(((bf16[16,1,512,256]{3,2,1,0:T(8,128)(2,1)}), bf16[16,1,512,256]{3,2,1,0:T(8,128)(2,1)}, u32[]{:S(2)}, u32[]{:S(2)}) %all-to-all-start) | async-done | bytes 4194336 | tf_op jit(solution)/shard_map/all_to_all | solution.py:42
  118.5 2.9 %fusion.54 = (f32[256]{0:T(256)S(1)}, f32[16,256]{1,0:T(8,128)S(1)}) fusion(bf16[8192,256]{1,0:T(8,128)(2,1)} %bitcast.21, s32[8192]{0:T(1024)S(1)} %bitcast.182), kind=kOutput, calls=%fused_computation.119 | convolution fusion | flops 67243776 | bytes 4244480 | tf_op jit(solution)/shard_map/ncs,nsf->ncf/dot_general | solution.py:51
  122.8 5.2 %fusion.8 = f32[256,256]{0,1:T(8,128)S(1)} fusion(bf16[16,1,512,256]{3,2,1,0:T(8,128)(2,1)} %all-to-all-done), kind=kOutput, calls=%fused_computation.18 | convolution fusion | flops 1073741824 | bytes 4456448 | tf_op jit(solution)/shard_map/nsf,nsg->nfg/dot_general | solution.py:53
  128.0 1.1 fusion.7
  129.3 11.7 %custom-call.20 = f32[1,128,128]{2,1,0:T(8,128)S(1)} custom-call(f32[1,128,128]{2,1,0:T(8,128)S(1)} %cholesky.117), custom_call_target="Cholesky" | custom-call | tf_op jit(solution)/shard_map/jit(cholesky)/cholesky | solution.py:18
  141.0 9.8 %custom-call.21 = f32[1,1,128,128]{2,3,1,0:T(8,128)S(1)} custom-call(f32[1,1,128,128]{3,2,1,0:T(8,128)S(1)} %get-tuple-element.30), custom_call_target="InvertDiagBlocksLowerTriangular" | custom-call | tf_op jit(solution)/shard_map/jit(cholesky)/cholesky | solution.py:18
  151.3 11.9 %custom-call.22 = f32[1,128,128]{2,1,0:T(8,128)S(1)} custom-call(f32[1,128,128]{2,1,0:T(8,128)S(1)} %fusion.11), custom_call_target="Cholesky" | custom-call | tf_op jit(solution)/shard_map/jit(cholesky)/cholesky | solution.py:18
  165.9 3.9 %while.1 = (s32[]{:T(128)}, f32[1,256,256]{2,1,0:T(8,128)S(1)}, s32[2,2]{1,0:T(2,128)S(1)}, f32[2,1,128,128]{3,2,1,0:T(8,128)S(1)}, s32[]{:T(128)}) while((s32[]{:T(128)}, f32[1,256,256]{2,1,0:T(8,128)S(1)}, s32[2,2]{1,0:T(2,128)S(1)}, f32[2,1,128,128]{3,2,1,0:T(8,128)S(1)}, s32[]{:T(128)}) %tuple.32), condition=%wide.while_cond, body=%wide.while_body.sunk | while | flops 2 | bytes 131181 | solution.py:19
  166.5 1.4 bitcast_dynamic-update-slice_fusion.3
  168.5 1.4 bitcast_dynamic-update-slice_fusion.3
  169.8 19.7 %custom-call.23 = f32[1,2,128,128]{2,3,1,0:T(8,128)S(1)} custom-call(f32[1,2,128,128]{3,2,1,0:T(8,128)S(1)} %bitcast.188), custom_call_target="InvertDiagBlocksLowerTriangular" | custom-call | tf_op jit(solution)/shard_map/vmap(jit(_cho_solve))/triangular_solve | solution.py:19
  191.3 35.7 %all_gather.6 = bf16[16,16,256]{2,1,0:T(8,128)(2,1)S(1)} all-gather(bf16[1,16,256]{2,1,0:T(8,128)(2,1)S(1)} %get-tuple-element.21), channel_id=1, replica_groups=mesh['leaf'=2,'rows'=16] {'rows'}, dimensions={0}, use_global_device_ids=true | all-gather | bytes 139264 | tf_op jit(solution)/shard_map/all_gather | solution.py:56
  227.3 29.8 %all-reduce.1 = f32[256]{0:T(256)S(1)} all-reduce(f32[256]{0:T(256)S(1)} %dynamic-update-slice.11), channel_id=2, replica_groups=mesh['leaf'=2,'rows'=16] {'rows'}, use_global_device_ids=true, to_apply=%add.1 | all-reduce | flops 256 | bytes 2048
  257.2 3.4 %fusion.5 = f32[16,16,512]{2,0,1:T(8,128)S(1)} fusion(bf16[16,512,256]{2,1,0:T(8,128)(2,1)} %gather_fusion, pred[16]{0:T(512)(128)(4,1)S(1)} %get-tuple-element.35, f32[16,16]{0,1:T(8,128)S(1)} %bitcast.187, pred[16,512]{1,0:T(8,128)(4,1)S(1)} %get-tuple-element.24, bf16[16,16,256]{2,1,0:T(8,128)(2,1)S(1)} %all_gather.6), kind=kOutput, calls=%fused_computation.14 | convolution fusion | flops 69468160 | bytes 4858896 | tf_op jit(solution)/shard_map/ncf,nsf->cns/dot_general | solution.py:60
  261.3 0.8 broadcast_select_fusion.9
  (61 shorter events, 17.6 us)
Async XLA Ops:
  7.2 27.6 %all-to-all-start.1 = ((bf16[16,2,256]{2,1,0:T(2,128)(2,1)}), bf16[16,2,256]{2,1,0:T(2,128)(2,1)S(1)}, u32[]{:S(2)}, u32[]{:S(2)}) async-start(bf16[16,2,256]{2,1,0:T(2,128)(2,1)} %reshape.405), calls=%async_computation.1 | async-start | bytes 32768 | tf_op jit(solution)/shard_map/all_to_all | solution.py:47
  34.8 6.3 %copy-start = (u32[32]{0:T(128)S(1)}, u32[32]{0:T(128)}, u32[]{:S(2)}) copy-start(u32[32]{0:T(128)} %constant.166) | copy-start | bytes 388
  34.8 83.7 %all-to-all-start = ((bf16[16,1,512,256]{3,2,1,0:T(8,128)(2,1)}), bf16[16,1,512,256]{3,2,1,0:T(8,128)(2,1)}, u32[]{:S(2)}, u32[]{:S(2)}) async-start(bf16[16,1,512,256]{3,2,1,0:T(8,128)(2,1)} %fusion.17), calls=%async_computation | async-start | bytes 8388608 | tf_op jit(solution)/shard_map/all_to_all | solution.py:42
